TPU v7x, 32 devices: a whole 2x2x4 slice. The times are simulated.
32 devices in a mesh: groups: 2 (over x), seg: 16 (over z, y, core).
Axes of the slice: x: 2, y: 2, z: 4, core: 2. Of those that a mesh axis runs over, the one named last changes fastest.
Arguments:
- bins: bfloat16 [1024, 128], P(('groups', 'seg')), parts along dimension 0, may hold values from -6 to 6
- conv_weight: bfloat16 [3, 128, 128], replicated, may hold values from -0.3125 to 0.3125
- conv_bias: float32 [128], replicated, may hold values from -3 to 3
- pair_left: bfloat16 [128, 48], replicated, may hold values from -0.5 to 0.5
- pair_right: bfloat16 [128, 48], replicated, may hold values from -0.5 to 0.5
- pair_weight: bfloat16 [3, 3, 48, 48], replicated, may hold values from -0.3125 to 0.3125
- pair_bias: float32 [48], replicated, may hold values from -3 to 3
- head: bfloat16 [48], replicated, may hold values from -0.875 to 0.875
- shifts: int32 [4], replicated, may hold values from -8 to 8, as said below
- flags: int32 [4], replicated, may hold values from 0 to 1, as said below
- dilations: int32 [2], replicated, may hold values from 1 to 4, as said below
Outputs:
- contacts: float32 [1024, 512], P(('groups', 'seg')), parts along dimension 0
There are 2 independent parts, one for each index of `groups`. A program takes and returns all parts, laid end to end along the dimension named above; an argument that names none is the same for every part. Nothing has to cross between parts.
Inputs may be any that keep to these rules, and one draw needn't show every extreme that they name: `shifts`: the largest entry is 8 and the smallest -8. `flags`: exactly half of the views are reverse-complemented. `dilations`: one of the two rates equals 4 and the other is smaller.
All inputs are finite; a program needn't handle non-finite values.
Results may differ from a plain program's by a relative error of at most 0.0055.
Values may be sent and summed in bfloat16 or wider, within the bound.
A program may use at most 128 MiB of HBM per device.

v0:
```python
import jax
import jax.numpy as jnp
from jax import lax
from jax.sharding import PartitionSpec as P

CHANNELS = 128
PAIR_CH = 48
BAND = 512
VIEWS = 4
DMAX = 4
HALO = 12
AHEAD = 18


def extended(value, sides, width):
    for axis, dim in sides:
        size, length = (lax.axis_size(axis), value.shape[dim])
        up = [(i, (i + 1) % size) for i in range(size - 1)]
        down = [(j, i) for i, j in up]
        last = lax.slice_in_dim(value, length - width, length, axis=dim)
        leading = lax.slice_in_dim(value, 0, width, axis=dim)
        before = lax.ppermute(last, axis, up)
        after = lax.ppermute(leading, axis, down)
        value = jnp.concatenate([before, value, after], axis=dim)
    return value


def passed_along(block, axis, distance):
    devices = range(lax.axis_size(axis))
    route = [(i - distance, i) for i in devices if i - distance in devices]
    return lax.ppermute(block, axis, route)


def view_kernels(conv_weight, flags):
    flipped = conv_weight[::-1, ::-1, :]
    chosen = (flags == 1)[:, None, None, None]
    return jnp.where(chosen, flipped[None], conv_weight[None])


def trunk(source, base, rows, shifts, dilate_seq, kernels, conv_bias, pair_left, pair_right):

    def one_view(shift, kernel):
        start = base + shift
        taps = [
            lax.dynamic_slice_in_dim(source, start + (tap - 1) * dilate_seq, rows, 0)
            for tap in range(3)
        ]
        mixed = jnp.zeros((rows, CHANNELS), jnp.float32)
        for tap in range(3):
            mixed = mixed + jnp.dot(taps[tap], kernel[tap], preferred_element_type=jnp.float32)
        return (taps[1], mixed)

    centers, mixed = jax.vmap(one_view)(shifts, kernels)
    feature = (centers.astype(jnp.float32) + jax.nn.relu(mixed + conv_bias)).astype(jnp.bfloat16)
    left = jnp.einsum("vrc,cp->vrp", feature, pair_left, preferred_element_type=jnp.float32).astype(
        jnp.bfloat16
    )
    right = jnp.einsum(
        "vrc,cp->vrp", feature, pair_right, preferred_element_type=jnp.float32
    ).astype(jnp.bfloat16)
    return (left, right)


def pair_block(left_rows, right_rows, first_row, total, dilate_pair, pair_weight, pair_bias, head):
    span = left_rows.shape[1]
    rows_out = span - 2 * DMAX
    width = right_rows.shape[1]
    global_rows = first_row + jnp.arange(span, dtype=jnp.int32)
    offsets = jnp.arange(BAND, dtype=jnp.int32)
    inside = ((global_rows >= 0) & (global_rows < total))[:, None] & (
        global_rows[:, None] + offsets[None, :] < total
    )
    head_float = head.astype(jnp.float32)
    padded_width = BAND + 2 * DMAX

    def view_step(view, running):
        left = left_rows[view]
        right_cols = right_rows[view].T
        skewed = jnp.tile(right_cols, (1, span + 1))[:, : span * (width + 1)]
        skewed = skewed.reshape(PAIR_CH, span, width + 1)[:, :, :BAND]
        pairs = jax.nn.relu(left.T.astype(jnp.float32)[:, :, None] + skewed.astype(jnp.float32))
        pairs = jnp.where(inside[None], pairs, 0.0).astype(jnp.bfloat16)
        padded = jnp.pad(pairs, ((0, 0), (0, 0), (DMAX, DMAX)))
        summed = jnp.zeros((PAIR_CH, rows_out, BAND), jnp.float32)
        for row_tap in range(3):
            row_start = DMAX + (row_tap - 1) * dilate_pair
            row_piece = lax.dynamic_slice(
                padded, (jnp.int32(0), row_start, jnp.int32(0)), (PAIR_CH, rows_out, padded_width)
            )
            product = jnp.einsum(
                "cid,bce->beid", row_piece, pair_weight[row_tap], preferred_element_type=jnp.float32
            )
            for col_tap in range(3):
                col_start = DMAX + (col_tap - 1) * dilate_pair
                summed = summed + lax.dynamic_slice(
                    product[col_tap],
                    (jnp.int32(0), jnp.int32(0), col_start),
                    (PAIR_CH, rows_out, BAND),
                )
        hidden = jax.nn.relu(summed + pair_bias[:, None, None])
        return running + jnp.einsum("eid,e->id", hidden, head_float)

    running = lax.fori_loop(0, VIEWS, view_step, jnp.zeros((rows_out, BAND), jnp.float32))
    return running / VIEWS


def per_device(
    bins,
    conv_weight,
    conv_bias,
    pair_left,
    pair_right,
    pair_weight,
    pair_bias,
    head,
    shifts,
    flags,
    dilations,
):
    rows = bins.shape[0]
    segments = lax.axis_size("seg")
    position = lax.axis_index("seg")
    total = rows * segments
    kernels = view_kernels(conv_weight, flags)
    span = rows + 2 * DMAX
    rim = extended(bins, (("seg", 0),), HALO)
    left, right = trunk(
        rim, HALO, rows, shifts, dilations[0], kernels, conv_bias, pair_left, pair_right
    )
    carried = (
        jnp.concatenate([left, right], 2).transpose(1, 0, 2).reshape(rows, VIEWS * 2 * PAIR_CH)
    )
    behind = passed_along(carried, "seg", 1)
    front = carried
    reached = 1
    for step in range(AHEAD.bit_length() - 1):
        front = jnp.concatenate([front, passed_along(front, "seg", -reached)], 0)
        reached = reached * 2
    tail_rows = front[: (AHEAD - reached) * rows]
    front = jnp.concatenate([front, passed_along(tail_rows, "seg", -reached)], 0)
    window = jnp.concatenate([behind, front], 0)
    first = rows - DMAX
    grouped = window.reshape(-1, VIEWS, 2 * PAIR_CH).transpose(1, 0, 2)
    left_rows = grouped[:, first : first + span, :PAIR_CH]
    right_rows = grouped[:, first : first + span + BAND, PAIR_CH:]
    return pair_block(
        left_rows,
        right_rows,
        position * rows - DMAX,
        total,
        dilations[1],
        pair_weight,
        pair_bias,
        head,
    )


def solution(mesh):
    placed = (P(("groups", "seg"), None), P(), P(), P(), P(), P(), P(), P(), P(), P(), P())
    return jax.shard_map(
        per_device,
        mesh=mesh,
        in_specs=placed,
        out_specs=P(("groups", "seg"), None),
        check_vma=False,
    )
```

profile of v0, /device:TPU:0, one launch (start us, length us, event | category | flops | bytes accessed | tf_op | source)
XLA Modules:
  0.0 355.3 jit_solution(715674938283093827)
XLA Ops:
  0.8 2.4 collective-permute-start
  5.8 1.6 rev.3
  11.8 5.1 %while.21 = (s32[]{:T(128)}, bf16[56,128]{1,0:T(8,128)(2,1)S(1)}, s32[4,2]{0,1:T(2,128)S(1)}, bf16[4,32,128]{2,1,0:T(8,128)(2,1)S(1)}, s32[]{:T(128)}) while((s32[]{:T(128)}, bf16[56,128]{1,0:T(8,128)(2,1)S(1)}, s32[4,2]{0,1:T(2,128)S(1)}, bf16[4,32,128]{2,1,0:T(8,128)(2,1)S(1)}, s32[]{:T(128)}) %tuple.95), condition=%wide.while_cond.1, body=%wide.while_body.1.sunk | while | flops 2 | bytes 16481 | solution.py:45
  16.9 5.1 %while.20 = (s32[]{:T(128)}, bf16[56,128]{1,0:T(8,128)(2,1)S(1)}, s32[4,2]{0,1:T(2,128)S(1)}, bf16[4,32,128]{2,1,0:T(8,128)(2,1)S(1)}, s32[]{:T(128)}) while((s32[]{:T(128)}, bf16[56,128]{1,0:T(8,128)(2,1)S(1)}, s32[4,2]{0,1:T(2,128)S(1)}, bf16[4,32,128]{2,1,0:T(8,128)(2,1)S(1)}, s32[]{:T(128)}) %tuple.107), condition=%wide.while_cond, body=%wide.while_body.sunk | while | flops 2 | bytes 16481 | solution.py:45
  22.0 5.1 %while.22 = (s32[]{:T(128)}, bf16[56,128]{1,0:T(8,128)(2,1)S(1)}, s32[4,2]{0,1:T(2,128)S(1)}, bf16[4,32,128]{2,1,0:T(8,128)(2,1)S(1)}, s32[]{:T(128)}) while((s32[]{:T(128)}, bf16[56,128]{1,0:T(8,128)(2,1)S(1)}, s32[4,2]{0,1:T(2,128)S(1)}, bf16[4,32,128]{2,1,0:T(8,128)(2,1)S(1)}, s32[]{:T(128)}) %tuple.108), condition=%wide.while_cond.2, body=%wide.while_body.2.sunk | while | flops 2 | bytes 16481 | solution.py:45
  30.7 4.5 %collective-permute-done.3 = bf16[32,384]{1,0:T(8,128)(2,1)S(1)} collective-permute-done((bf16[32,384]{1,0:T(8,128)(2,1)S(1)}, bf16[32,384]{1,0:T(8,128)(2,1)S(1)}, u32[]{:S(2)}, u32[]{:S(2)}) %collective-permute-start.3) | collective-permute-done | bytes 24608 | tf_op jit(solution)/shard_map/ppermute | solution.py:31
  36.6 5.1 %collective-permute-done.4 = bf16[64,384]{1,0:T(8,128)(2,1)S(1)} collective-permute-done((bf16[64,384]{1,0:T(8,128)(2,1)S(1)}, bf16[64,384]{1,0:T(8,128)(2,1)S(1)}, u32[]{:S(2)}, u32[]{:S(2)}) %collective-permute-start.4) | collective-permute-done | bytes 49184 | tf_op jit(solution)/shard_map/ppermute | solution.py:31
  43.0 6.9 %collective-permute-done.5 = bf16[128,384]{1,0:T(8,128)(2,1)S(1)} collective-permute-done((bf16[128,384]{1,0:T(8,128)(2,1)S(1)}, bf16[128,384]{1,0:T(8,128)(2,1)S(1)}, u32[]{:S(2)}, u32[]{:S(2)}) %collective-permute-start.5) | collective-permute-done | bytes 98336 | tf_op jit(solution)/shard_map/ppermute | solution.py:31
  51.3 1.7 collective-permute-start.2
  56.4 1.6 copy.27
  58.8 4.8 %collective-permute-done.6 = bf16[256,384]{1,0:T(8,128)(2,1)S(1)} collective-permute-done((bf16[256,384]{1,0:T(8,128)(2,1)S(1)}, bf16[256,384]{1,0:T(8,128)(2,1)S(1)}, u32[]{:S(2)}, u32[]{:S(2)}) %collective-permute-start.6) | collective-permute-done | bytes 196640 | tf_op jit(solution)/shard_map/ppermute | solution.py:31
  65.3 288.5 %while.23 = (s32[]{:T(128)}, f32[32,512]{1,0:T(8,128)}, bf16[4,40,48]{2,1,0:T(8,128)(2,1)S(1)}, bf16[4,552,48]{1,2,0:T(8,128)(2,1)}, s32[]{:T(128)}, /*index=5*/...) while((s32[]{:T(128)}, f32[32,512]{1,0:T(8,128)}, ...), condition=%wide.region_1.2_spmd.clone, body=%wide.region_0.1_spmd.clone.sunk | while | flops 704542592 | bytes 148727280 | solution.py:103
  66.4 3.4 tile.30
  69.8 1.6 slice-done
  71.4 4.2 %reshape.173 = bf16[48,40,553]{2,1,0:T(8,128)(2,1)} reshape(bf16[48,22120]{1,0:T(8,128)(2,1)S(1)} %slice-done) | data formatting | bytes 4247040 | tf_op jit(solution)/shard_map/while/body/eval_jaxpr/reshape | solution.py:80
  78.3 6.1 %convolution_bitcast_fusion.7 = f32[3,48,32,520]{3,1,2,0:T(8,128)} fusion(s32[]{:T(128)} %get-tuple-element.731, bf16[48,40,512]{2,0,1:T(8,128)(2,1)S(1)} %select_convert_fusion.2, bf16[3,3,48,48]{2,3,1,0:T(8,128)(2,1)S(1)} %copy-done.2), kind=kOutput, calls=%fused_computation.7.clone.1 | convolution fusion | flops 230031360 | bytes 11587588 | tf_op jit(solution)/shard_map/while/body/eval_jaxpr/cid,bce->beid/dot_general | solution.py:90
  84.4 6.1 %convolution_bitcast_fusion.6 = f32[3,48,32,520]{3,1,2,0:T(8,128)} fusion(bf16[48,40,512]{2,0,1:T(8,128)(2,1)S(1)} %select_convert_fusion.2, bf16[3,3,48,48]{2,3,1,0:T(8,128)(2,1)S(1)} %copy-done.2), kind=kOutput, calls=%fused_computation.8.clone.1 | convolution fusion | flops 230031360 | bytes 11587584 | tf_op jit(solution)/shard_map/while/body/eval_jaxpr/cid,bce->beid/dot_general | solution.py:90
  90.4 13.8 %fusion.89 = (f32[1,48,32,520]{3,1,2,0:T(8,128)S(1)}, f32[1,48,32,520]{3,1,2,0:T(8,128)S(1)}, f32[48,32,520]{2,0,1:T(8,128)}, f32[48,32,520]{2,0,1:T(8,128)}, f3...) fusion(f32[3,48,32,520]{3,1,2,0:T(8,128)} %convolution_bitcast_fusion.6, ...), kind=kLoop, calls=%fused_computation.97.clone.1 | loop fusion | bytes 38338560 | tf_op jit(solution)/shard_map/while/body/eval_jaxpr/slice | solution.py:96
  104.2 6.9 %convolution_bitcast_fusion.8 = f32[3,48,32,520]{3,1,0,2:T(8,128)} fusion(s32[]{:T(128)} %get-tuple-element.727, bf16[48,40,512]{2,0,1:T(8,128)(2,1)S(1)} %select_convert_fusion.2, bf16[3,3,48,48]{2,3,1,0:T(8,128)(2,1)} %get-tuple-element.728), kind=kOutput, calls=%fused_computation.9.clone.1 | convolution fusion | flops 230031360 | bytes 11588096 | tf_op jit(solution)/shard_map/while/body/eval_jaxpr/cid,bce->beid/dot_general | solution.py:90
  111.1 9.0 %fusion.90 = (f32[1,48,32,520]{3,1,0,2:T(8,128)}, f32[1,48,32,520]{3,1,0,2:T(8,128)}, f32[48,32,520]{2,0,1:T(8,128)}) fusion(f32[3,48,32,520]{3,1,0,2:T(8,128)} %convolution_bitcast_fusion.8), kind=kLoop, calls=%fused_computation.96.clone.1 | loop fusion | bytes 19169280 | tf_op jit(solution)/shard_map/while/body/eval_jaxpr/slice | solution.py:96
  120.1 16.7 %fusion.91 = f32[1,32,512]{2,0,1:T(1,128)S(1)} fusion(f32[48,32,520]{2,0,1:T(8,128)} %get-tuple-element.639, f32[48,32,520]{2,0,1:T(8,128)} %get-tuple-element.640, f32[48,32,520]{2,0,1:T(8,128)} %get-tuple-element.641, f32[1,48,32,520]{3,1,2,0:T(8,128)} %get-tuple-element.642, s32[]{:T(128)} %get-tuple-element.730, ...), kind=kOutput, calls=%fused_computation.18.clone.1 | convolution fusion | flops 9437184 | bytes 28379136 | tf_op jit(solution)/shard_map/while/body/eval_jaxpr/eid,e->id/dot_general | solution.py:101
  138.5 3.4 tile.30
  141.9 1.6 slice-done
  143.5 4.2 %reshape.173 = bf16[48,40,553]{2,1,0:T(8,128)(2,1)} reshape(bf16[48,22120]{1,0:T(8,128)(2,1)S(1)} %slice-done) | data formatting | bytes 4247040 | tf_op jit(solution)/shard_map/while/body/eval_jaxpr/reshape | solution.py:80
  150.4 6.1 %convolution_bitcast_fusion.7 = f32[3,48,32,520]{3,1,2,0:T(8,128)} fusion(s32[]{:T(128)} %get-tuple-element.731, bf16[48,40,512]{2,0,1:T(8,128)(2,1)S(1)} %select_convert_fusion.2, bf16[3,3,48,48]{2,3,1,0:T(8,128)(2,1)S(1)} %copy-done.2), kind=kOutput, calls=%fused_computation.7.clone.1 | convolution fusion | flops 230031360 | bytes 11587588 | tf_op jit(solution)/shard_map/while/body/eval_jaxpr/cid,bce->beid/dot_general | solution.py:90
  156.5 6.1 %convolution_bitcast_fusion.6 = f32[3,48,32,520]{3,1,2,0:T(8,128)} fusion(bf16[48,40,512]{2,0,1:T(8,128)(2,1)S(1)} %select_convert_fusion.2, bf16[3,3,48,48]{2,3,1,0:T(8,128)(2,1)S(1)} %copy-done.2), kind=kOutput, calls=%fused_computation.8.clone.1 | convolution fusion | flops 230031360 | bytes 11587584 | tf_op jit(solution)/shard_map/while/body/eval_jaxpr/cid,bce->beid/dot_general | solution.py:90
  162.5 13.8 %fusion.89 = (f32[1,48,32,520]{3,1,2,0:T(8,128)S(1)}, f32[1,48,32,520]{3,1,2,0:T(8,128)S(1)}, f32[48,32,520]{2,0,1:T(8,128)}, f32[48,32,520]{2,0,1:T(8,128)}, f3...) fusion(f32[3,48,32,520]{3,1,2,0:T(8,128)} %convolution_bitcast_fusion.6, ...), kind=kLoop, calls=%fused_computation.97.clone.1 | loop fusion | bytes 38338560 | tf_op jit(solution)/shard_map/while/body/eval_jaxpr/slice | solution.py:96
  176.3 6.9 %convolution_bitcast_fusion.8 = f32[3,48,32,520]{3,1,0,2:T(8,128)} fusion(s32[]{:T(128)} %get-tuple-element.727, bf16[48,40,512]{2,0,1:T(8,128)(2,1)S(1)} %select_convert_fusion.2, bf16[3,3,48,48]{2,3,1,0:T(8,128)(2,1)} %get-tuple-element.728), kind=kOutput, calls=%fused_computation.9.clone.1 | convolution fusion | flops 230031360 | bytes 11588096 | tf_op jit(solution)/shard_map/while/body/eval_jaxpr/cid,bce->beid/dot_general | solution.py:90
  183.2 9.0 %fusion.90 = (f32[1,48,32,520]{3,1,0,2:T(8,128)}, f32[1,48,32,520]{3,1,0,2:T(8,128)}, f32[48,32,520]{2,0,1:T(8,128)}) fusion(f32[3,48,32,520]{3,1,0,2:T(8,128)} %convolution_bitcast_fusion.8), kind=kLoop, calls=%fused_computation.96.clone.1 | loop fusion | bytes 19169280 | tf_op jit(solution)/shard_map/while/body/eval_jaxpr/slice | solution.py:96
  192.2 16.7 %fusion.91 = f32[1,32,512]{2,0,1:T(1,128)S(1)} fusion(f32[48,32,520]{2,0,1:T(8,128)} %get-tuple-element.639, f32[48,32,520]{2,0,1:T(8,128)} %get-tuple-element.640, f32[48,32,520]{2,0,1:T(8,128)} %get-tuple-element.641, f32[1,48,32,520]{3,1,2,0:T(8,128)} %get-tuple-element.642, s32[]{:T(128)} %get-tuple-element.730, ...), kind=kOutput, calls=%fused_computation.18.clone.1 | convolution fusion | flops 9437184 | bytes 28379136 | tf_op jit(solution)/shard_map/while/body/eval_jaxpr/eid,e->id/dot_general | solution.py:101
  210.6 3.4 tile.30
  214.0 1.6 slice-done
  215.6 4.2 %reshape.173 = bf16[48,40,553]{2,1,0:T(8,128)(2,1)} reshape(bf16[48,22120]{1,0:T(8,128)(2,1)S(1)} %slice-done) | data formatting | bytes 4247040 | tf_op jit(solution)/shard_map/while/body/eval_jaxpr/reshape | solution.py:80
  222.5 6.1 %convolution_bitcast_fusion.7 = f32[3,48,32,520]{3,1,2,0:T(8,128)} fusion(s32[]{:T(128)} %get-tuple-element.731, bf16[48,40,512]{2,0,1:T(8,128)(2,1)S(1)} %select_convert_fusion.2, bf16[3,3,48,48]{2,3,1,0:T(8,128)(2,1)S(1)} %copy-done.2), kind=kOutput, calls=%fused_computation.7.clone.1 | convolution fusion | flops 230031360 | bytes 11587588 | tf_op jit(solution)/shard_map/while/body/eval_jaxpr/cid,bce->beid/dot_general | solution.py:90
  228.6 6.1 %convolution_bitcast_fusion.6 = f32[3,48,32,520]{3,1,2,0:T(8,128)} fusion(bf16[48,40,512]{2,0,1:T(8,128)(2,1)S(1)} %select_convert_fusion.2, bf16[3,3,48,48]{2,3,1,0:T(8,128)(2,1)S(1)} %copy-done.2), kind=kOutput, calls=%fused_computation.8.clone.1 | convolution fusion | flops 230031360 | bytes 11587584 | tf_op jit(solution)/shard_map/while/body/eval_jaxpr/cid,bce->beid/dot_general | solution.py:90
  234.7 13.8 %fusion.89 = (f32[1,48,32,520]{3,1,2,0:T(8,128)S(1)}, f32[1,48,32,520]{3,1,2,0:T(8,128)S(1)}, f32[48,32,520]{2,0,1:T(8,128)}, f32[48,32,520]{2,0,1:T(8,128)}, f3...) fusion(f32[3,48,32,520]{3,1,2,0:T(8,128)} %convolution_bitcast_fusion.6, ...), kind=kLoop, calls=%fused_computation.97.clone.1 | loop fusion | bytes 38338560 | tf_op jit(solution)/shard_map/while/body/eval_jaxpr/slice | solution.py:96
  248.5 6.9 %convolution_bitcast_fusion.8 = f32[3,48,32,520]{3,1,0,2:T(8,128)} fusion(s32[]{:T(128)} %get-tuple-element.727, bf16[48,40,512]{2,0,1:T(8,128)(2,1)S(1)} %select_convert_fusion.2, bf16[3,3,48,48]{2,3,1,0:T(8,128)(2,1)} %get-tuple-element.728), kind=kOutput, calls=%fused_computation.9.clone.1 | convolution fusion | flops 230031360 | bytes 11588096 | tf_op jit(solution)/shard_map/while/body/eval_jaxpr/cid,bce->beid/dot_general | solution.py:90
  255.3 9.0 %fusion.90 = (f32[1,48,32,520]{3,1,0,2:T(8,128)}, f32[1,48,32,520]{3,1,0,2:T(8,128)}, f32[48,32,520]{2,0,1:T(8,128)}) fusion(f32[3,48,32,520]{3,1,0,2:T(8,128)} %convolution_bitcast_fusion.8), kind=kLoop, calls=%fused_computation.96.clone.1 | loop fusion | bytes 19169280 | tf_op jit(solution)/shard_map/while/body/eval_jaxpr/slice | solution.py:96
  264.3 16.7 %fusion.91 = f32[1,32,512]{2,0,1:T(1,128)S(1)} fusion(f32[48,32,520]{2,0,1:T(8,128)} %get-tuple-element.639, f32[48,32,520]{2,0,1:T(8,128)} %get-tuple-element.640, f32[48,32,520]{2,0,1:T(8,128)} %get-tuple-element.641, f32[1,48,32,520]{3,1,2,0:T(8,128)} %get-tuple-element.642, s32[]{:T(128)} %get-tuple-element.730, ...), kind=kOutput, calls=%fused_computation.18.clone.1 | convolution fusion | flops 9437184 | bytes 28379136 | tf_op jit(solution)/shard_map/while/body/eval_jaxpr/eid,e->id/dot_general | solution.py:101
  282.7 3.4 tile.30
  286.2 1.6 slice-done
  287.8 4.2 %reshape.173 = bf16[48,40,553]{2,1,0:T(8,128)(2,1)} reshape(bf16[48,22120]{1,0:T(8,128)(2,1)S(1)} %slice-done) | data formatting | bytes 4247040 | tf_op jit(solution)/shard_map/while/body/eval_jaxpr/reshape | solution.py:80
  294.6 6.1 %convolution_bitcast_fusion.7 = f32[3,48,32,520]{3,1,2,0:T(8,128)} fusion(s32[]{:T(128)} %get-tuple-element.731, bf16[48,40,512]{2,0,1:T(8,128)(2,1)S(1)} %select_convert_fusion.2, bf16[3,3,48,48]{2,3,1,0:T(8,128)(2,1)S(1)} %copy-done.2), kind=kOutput, calls=%fused_computation.7.clone.1 | convolution fusion | flops 230031360 | bytes 11587588 | tf_op jit(solution)/shard_map/while/body/eval_jaxpr/cid,bce->beid/dot_general | solution.py:90
  300.7 6.1 %convolution_bitcast_fusion.6 = f32[3,48,32,520]{3,1,2,0:T(8,128)} fusion(bf16[48,40,512]{2,0,1:T(8,128)(2,1)S(1)} %select_convert_fusion.2, bf16[3,3,48,48]{2,3,1,0:T(8,128)(2,1)S(1)} %copy-done.2), kind=kOutput, calls=%fused_computation.8.clone.1 | convolution fusion | flops 230031360 | bytes 11587584 | tf_op jit(solution)/shard_map/while/body/eval_jaxpr/cid,bce->beid/dot_general | solution.py:90
  306.8 13.8 %fusion.89 = (f32[1,48,32,520]{3,1,2,0:T(8,128)S(1)}, f32[1,48,32,520]{3,1,2,0:T(8,128)S(1)}, f32[48,32,520]{2,0,1:T(8,128)}, f32[48,32,520]{2,0,1:T(8,128)}, f3...) fusion(f32[3,48,32,520]{3,1,2,0:T(8,128)} %convolution_bitcast_fusion.6, ...), kind=kLoop, calls=%fused_computation.97.clone.1 | loop fusion | bytes 38338560 | tf_op jit(solution)/shard_map/while/body/eval_jaxpr/slice | solution.py:96
  320.6 6.9 %convolution_bitcast_fusion.8 = f32[3,48,32,520]{3,1,0,2:T(8,128)} fusion(s32[]{:T(128)} %get-tuple-element.727, bf16[48,40,512]{2,0,1:T(8,128)(2,1)S(1)} %select_convert_fusion.2, bf16[3,3,48,48]{2,3,1,0:T(8,128)(2,1)} %get-tuple-element.728), kind=kOutput, calls=%fused_computation.9.clone.1 | convolution fusion | flops 230031360 | bytes 11588096 | tf_op jit(solution)/shard_map/while/body/eval_jaxpr/cid,bce->beid/dot_general | solution.py:90
  327.4 9.0 %fusion.90 = (f32[1,48,32,520]{3,1,0,2:T(8,128)}, f32[1,48,32,520]{3,1,0,2:T(8,128)}, f32[48,32,520]{2,0,1:T(8,128)}) fusion(f32[3,48,32,520]{3,1,0,2:T(8,128)} %convolution_bitcast_fusion.8), kind=kLoop, calls=%fused_computation.96.clone.1 | loop fusion | bytes 19169280 | tf_op jit(solution)/shard_map/while/body/eval_jaxpr/slice | solution.py:96
  336.4 16.7 %fusion.91 = f32[1,32,512]{2,0,1:T(1,128)S(1)} fusion(f32[48,32,520]{2,0,1:T(8,128)} %get-tuple-element.639, f32[48,32,520]{2,0,1:T(8,128)} %get-tuple-element.640, f32[48,32,520]{2,0,1:T(8,128)} %get-tuple-element.641, f32[1,48,32,520]{3,1,2,0:T(8,128)} %get-tuple-element.642, s32[]{:T(128)} %get-tuple-element.730, ...), kind=kOutput, calls=%fused_computation.18.clone.1 | convolution fusion | flops 9437184 | bytes 28379136 | tf_op jit(solution)/shard_map/while/body/eval_jaxpr/eid,e->id/dot_general | solution.py:101
  (153 shorter events, 51.9 us)
Async XLA Ops:
  0.0 28.2 %copy-start = (bf16[128,48]{0,1:T(8,128)(2,1)S(1)}, bf16[128,48]{0,1:T(8,128)(2,1)}, u32[]{:S(2)}) copy-start(bf16[128,48]{0,1:T(8,128)(2,1)} %param.17) | copy-start | bytes 36868
  0.0 65.3 %copy-start.5 = (f32[48]{0:T(128)S(1)}, f32[48]{0:T(128)}, u32[]{:S(2)}) copy-start(f32[48]{0:T(128)} %param.19) | copy-start | bytes 580
  0.0 65.3 %copy-start.6 = (bf16[48]{0:T(256)(128)(2,1)S(1)}, bf16[48]{0:T(256)(128)(2,1)}, u32[]{:S(2)}) copy-start(bf16[48]{0:T(256)(128)(2,1)} %param.20) | copy-start | bytes 292
  0.8 10.3 %collective-permute-start = (bf16[12,128]{1,0:T(8,128)(2,1)S(1)}, bf16[12,128]{1,0:T(8,128)(2,1)S(1)}, u32[]{:S(2)}, u32[]{:S(2)}) collective-permute-start(bf16[12,128]{1,0:T(8,128)(2,1)S(1)} %get-tuple-element.469), channel_id=1, source_target_pairs={{0,1},{1,2},{2,3},{3,4},{4,5},{5,6},{6,7},{7,8},{8,9},{9,10},{10,1... | collective-permute-start | bytes 9224 | tf_op jit(solution)/shard_map/ppermute | solution.py:22
  3.1 7.9 %collective-permute-start.1 = (bf16[12,128]{1,0:T(8,128)(2,1)S(1)}, bf16[12,128]{1,0:T(8,128)(2,1)S(1)}, u32[]{:S(2)}, u32[]{:S(2)}) collective-permute-start(bf16[12,128]{1,0:T(8,128)(2,1)S(1)} %get-tuple-element.470), channel_id=1, source_target_pairs={{1,0},{2,1},{3,2},{4,3},{5,4},{6,5},{7,6},{8,7},{9,8},{10,9},{11,1... | collective-permute-start | bytes 9224 | tf_op jit(solution)/shard_map/ppermute | solution.py:23
  29.4 5.8 %collective-permute-start.3 = (bf16[32,384]{1,0:T(8,128)(2,1)S(1)}, bf16[32,384]{1,0:T(8,128)(2,1)S(1)}, u32[]{:S(2)}, u32[]{:S(2)}) collective-permute-start(bf16[32,384]{1,0:T(8,128)(2,1)S(1)} %reshape.101), channel_id=1, source_target_pairs={{1,0},{2,1},{3,2},{4,3},{5,4},{6,5},{7,6},{8,7},{9,8},{10,9},{11,1... | collective-permute-start | bytes 73736 | tf_op jit(solution)/shard_map/ppermute | solution.py:31
  35.3 6.4 %collective-permute-start.4 = (bf16[64,384]{1,0:T(8,128)(2,1)S(1)}, bf16[64,384]{1,0:T(8,128)(2,1)S(1)}, u32[]{:S(2)}, u32[]{:S(2)}) collective-permute-start(bf16[64,384]{1,0:T(8,128)(2,1)S(1)} %constant_dynamic-update-slice_fusion), channel_id=1, source_target_pairs={{2,0},{3,1},{4,2},{5,3},{6,4},{7,5},{8,6},{9,7},{10,8},{11,9},{12,... | collective-permute-start | bytes 147464 | tf_op jit(solution)/shard_map/ppermute | solution.py:31
  41.7 8.2 %collective-permute-start.5 = (bf16[128,384]{1,0:T(8,128)(2,1)S(1)}, bf16[128,384]{1,0:T(8,128)(2,1)S(1)}, u32[]{:S(2)}, u32[]{:S(2)}) collective-permute-start(bf16[128,384]{1,0:T(8,128)(2,1)S(1)} %pad_maximum_fusion.1), channel_id=1, source_target_pairs={{4,0},{5,1},{6,2},{7,3},{8,4},{9,5},{10,6},{11,7},{12,8},{13,9},{1... | collective-permute-start | bytes 294920 | tf_op jit(solution)/shard_map/ppermute | solution.py:31
  50.0 13.6 %collective-permute-start.6 = (bf16[256,384]{1,0:T(8,128)(2,1)S(1)}, bf16[256,384]{1,0:T(8,128)(2,1)S(1)}, u32[]{:S(2)}, u32[]{:S(2)}) collective-permute-start(bf16[256,384]{1,0:T(8,128)(2,1)S(1)} %pad_maximum_fusion), channel_id=1, source_target_pairs={{8,0},{9,1},{10,2},{11,3},{12,4},{13,5},{14,6},{15,7},{24,16},{25,... | collective-permute-start | bytes 589832 | tf_op jit(solution)/shard_map/ppermute | solution.py:31
  51.3 7.0 %collective-permute-start.2 = (bf16[32,384]{1,0:T(8,128)(2,1)S(1)}, bf16[32,384]{1,0:T(8,128)(2,1)S(1)}, u32[]{:S(2)}, u32[]{:S(2)}) collective-permute-start(bf16[32,384]{1,0:T(8,128)(2,1)S(1)} %reshape.101), channel_id=1, source_target_pairs={{0,1},{1,2},{2,3},{3,4},{4,5},{5,6},{6,7},{7,8},{8,9},{9,10},{10,1... | collective-permute-start | bytes 73736 | tf_op jit(solution)/shard_map/ppermute | solution.py:31
  52.9 5.6 %collective-permute-start.7 = (bf16[64,384]{1,0:T(8,128)(2,1)S(1)}, bf16[64,384]{1,0:T(8,128)(2,1)S(1)}, u32[]{:S(2)}, u32[]{:S(2)}) collective-permute-start(bf16[64,384]{1,0:T(8,128)(2,1)S(1)} %constant_dynamic-update-slice_fusion), channel_id=1, source_target_pairs={} | collective-permute-start | bytes 147464 | tf_op jit(solution)/shard_map/ppermute | solution.py:31
  69.8 1.6 slice-start
  75.6 1.5 slice-start.1
  75.6 2.7 copy-start.2
  120.1 16.7 %copy-start.3 = (f32[32,512]{1,0:T(8,128)S(1)}, f32[32,512]{1,0:T(8,128)}, u32[]{:S(2)}) copy-start(f32[32,512]{1,0:T(8,128)} %get-tuple-element.709) | copy-start | bytes 196612 | tf_op jit(solution)/shard_map/while
  136.8 0.6 copy-start.4
  141.9 1.6 slice-start
  147.7 1.5 slice-start.1
  147.7 2.7 copy-start.2
  192.2 16.7 %copy-start.3 = (f32[32,512]{1,0:T(8,128)S(1)}, f32[32,512]{1,0:T(8,128)}, u32[]{:S(2)}) copy-start(f32[32,512]{1,0:T(8,128)} %get-tuple-element.709) | copy-start | bytes 196612 | tf_op jit(solution)/shard_map/while
  208.9 0.6 copy-start.4
  214.0 1.6 slice-start
  219.8 1.5 slice-start.1
  219.8 2.7 copy-start.2
  264.3 16.7 %copy-start.3 = (f32[32,512]{1,0:T(8,128)S(1)}, f32[32,512]{1,0:T(8,128)}, u32[]{:S(2)}) copy-start(f32[32,512]{1,0:T(8,128)} %get-tuple-element.709) | copy-start | bytes 196612 | tf_op jit(solution)/shard_map/while
  281.0 0.6 copy-start.4
  286.2 1.6 slice-start
  291.9 1.5 slice-start.1
  291.9 2.7 copy-start.2
  336.4 16.7 %copy-start.3 = (f32[32,512]{1,0:T(8,128)S(1)}, f32[32,512]{1,0:T(8,128)}, u32[]{:S(2)}) copy-start(f32[32,512]{1,0:T(8,128)} %get-tuple-element.709) | copy-start | bytes 196612 | tf_op jit(solution)/shard_map/while
  353.1 0.6 copy-start.4
  353.8 1.5 copy-start.1
where the time goes:
time: 357 us; the launch traced here: 355 us
  local copies, waits for them, and re-layouts  164 us (46%)
  matrix products  145 us (41%)
  waiting for transfers between devices  21.4 us (6%)
  starting transfers between devices  11.1 us (3%)
  other arithmetic  10.3 us (3%)
  between operations  3.65 us (1%)
    slice x8, local copies, waits for them, and re-layouts, view_step(): product[col_tap]  91.1 us
    dot_general x12, matrix products, view_step(): jnp.einsum('cid,bce->beid', row_piece, pair_weight[row_tap], preferred_el...  76 us
    dot_general x4, matrix products, view_step(): return running + jnp.einsum('eid,e->id', hidden, head_float)  66.8 us
    ppermute x6, waiting for transfers between devices, passed_along(): return lax.ppermute(block, axis, route)  21.4 us
    reshape x4, local copies, waits for them, and re-layouts, view_step(): skewed = skewed.reshape(PAIR_CH, span, width + 1)[:, :, :BAND]  16.7 us
    gather x36, local copies, waits for them, and re-layouts  15.1 us
    another operation x8, local copies, waits for them, and re-layouts, view_step(): skewed = jnp.tile(right_cols, (1, span + 1))[:, :span * (width + 1)]  14.7 us
    ppermute x6, starting transfers between devices, passed_along(): return lax.ppermute(block, axis, route)  7.47 us
  transfers between devices with their start and end apart: 8, of which 4 were waited for; matrix products, arithmetic and copies ran while one was open for 2% of the time, Pallas kernels for 0%

commit v1 on v0

v1 whole, which is shorter than its diff:
```python
import functools

import jax
import jax.numpy as jnp
from jax import lax
from jax.experimental import pallas as pl
from jax.experimental.pallas import tpu as pltpu
from jax.sharding import PartitionSpec as P

BAND = 512
DMAX = 4
OUT_ROWS = 3
IN_ROWS = OUT_ROWS + 2
WIDE = 256
LEAD = 16
TILE = 16
FAR = -1e30
F32 = jnp.float32
BF16 = jnp.bfloat16


def gather_kernel(segments, blocks, rows, x_ref, out_ref, send_sem, recv_sem, own_sem):
    me = lax.axis_index("seg")
    barrier = pltpu.get_barrier_semaphore()
    reach = min(blocks - 2, segments - 1)
    count = jnp.int32(0)
    for step in range(1, reach + 1):
        for other in (me - step, me + step):
            there = (other >= 0) & (other < segments)

            @pl.when(there)
            def _():
                pl.semaphore_signal(
                    barrier,
                    inc=1,
                    device_id={"seg": other},
                    device_id_type=pl.DeviceIdType.MESH,
                )

            count = count + there.astype(jnp.int32)
    own = pltpu.make_async_copy(x_ref, out_ref.at[pl.ds(rows, rows)], own_sem)
    own.start()
    for slot in range(blocks):
        source = me + slot - 1

        @pl.when((source < 0) | (source >= segments))
        def _():
            out_ref[pl.ds(slot * rows, rows), :] = jnp.zeros((rows, out_ref.shape[1]), BF16)

    pl.semaphore_wait(barrier, count)

    def copy(slot):
        return pltpu.make_async_remote_copy(
            src_ref=x_ref,
            dst_ref=out_ref.at[pl.ds(slot * rows, rows)],
            send_sem=send_sem.at[slot],
            recv_sem=recv_sem.at[slot],
            device_id={"seg": me - slot + 1},
            device_id_type=pl.DeviceIdType.MESH,
        )

    for slot in reversed(range(blocks)):
        target = me - slot + 1
        if slot != 1 and abs(slot - 1) <= reach:

            @pl.when((target >= 0) & (target < segments))
            def _():
                copy(slot).start()

    own.wait()
    for slot in range(blocks):
        target = me - slot + 1
        source = me + slot - 1
        if slot != 1 and abs(slot - 1) <= reach:

            @pl.when((source >= 0) & (source < segments))
            def _():
                copy(slot).wait_recv()

            @pl.when((target >= 0) & (target < segments))
            def _():
                copy(slot).wait_send()


def slot_of(index, size):
    total = jnp.zeros(index.shape, jnp.int32)
    for k in range(1, IN_ROWS):
        total = total + (index >= k * size).astype(jnp.int32)
    return total


def dot(a, b, **kw):
    return jnp.dot(a, b, preferred_element_type=F32, **kw)


def pair_kernel(
    rows,
    segments,
    shifts,
    flags,
    dilations,
    win_ref,
    cw_ref,
    cb_ref,
    pleft_ref,
    pright_ref,
    pw_ref,
    pb_ref,
    head_ref,
    out_ref,
    xf,
    kern,
    wall,
    rt,
    r5,
    r5b,
    l5,
    cols,
):
    channels = win_ref.shape[1]
    pc = pleft_ref.shape[1]
    views = shifts.shape[0]
    total = rows * segments
    base = lax.axis_index("seg") * rows
    near = rows + BAND
    frows = near + 2 * LEAD
    q = dilations[0]
    r = dilations[1]

    xf[...] = win_ref[...].astype(F32)
    ci = lax.broadcasted_iota(jnp.int32, (channels, channels), 0)
    cj = lax.broadcasted_iota(jnp.int32, (channels, channels), 1)
    mirror = jnp.where(ci + cj == channels - 1, 1.0, 0.0).astype(BF16)
    for t in range(3):
        at = slice(t * channels, (t + 1) * channels)
        kern[0, at, :] = cw_ref[t]
        kern[1, at, :] = dot(mirror, cw_ref[2 - t]).astype(BF16)

    lane = lax.broadcasted_iota(jnp.int32, (pc, WIDE), 1)
    chan = lax.broadcasted_iota(jnp.int32, (pc, WIDE), 0)
    spots = [jnp.where(lane - chan == k * pc, 1.0, 0.0) for k in range(IN_ROWS)]
    tiler_f = sum(spots[1:], spots[0])
    tiler = tiler_f.astype(BF16)
    wide_left = dot(pleft_ref[...], tiler).astype(BF16)
    wide_right = dot(pright_ref[...], tiler).astype(BF16)
    placed = [dot(pw_ref[...], spots[o].astype(BF16)) for o in range(OUT_ROWS)]
    for b in range(3):
        for k in range(IN_ROWS):
            block = jnp.zeros((pc, WIDE), F32)
            for o in range(OUT_ROWS):
                if 0 <= k - o <= 2:
                    first = ((k - o) * 3 + b) * pc
                    block = block + placed[o][first : first + pc]
            wall[b * WIDE + k * pc : b * WIDE + (k + 1) * pc, :] = block.astype(BF16)
        wall[b * WIDE + IN_ROWS * pc : (b + 1) * WIDE, :] = jnp.zeros(
            (WIDE - IN_ROWS * pc, WIDE), BF16
        )
    bias8 = jnp.broadcast_to(pb_ref[...], (8, pc))
    bias = dot(bias8, tiler_f, precision=lax.Precision.HIGHEST)[0:1, :]
    wi = lax.broadcasted_iota(jnp.int32, (WIDE, pc), 0)
    wc = lax.broadcasted_iota(jnp.int32, (WIDE, pc), 1)
    hit = wi == wc
    for o in range(1, OUT_ROWS):
        hit = hit | (wi - wc == o * pc)
    untile = jnp.where(hit, 1.0, 0.0).astype(BF16)
    head_b = jnp.broadcast_to(head_ref[...].astype(F32), (128, pc)).astype(BF16)
    head_rows = lax.dot_general(
        untile, head_b, (((1,), (1,)), ((), ())), preferred_element_type=F32
    )
    target = lax.broadcasted_iota(jnp.int32, (WIDE, 128), 1) - r * slot_of(
        lax.broadcasted_iota(jnp.int32, (WIDE, 128), 0), pc
    )

    half = lax.broadcasted_iota(jnp.int32, (1, 128), 1)

    def skew(rows_out, first):
        def at(k, side):
            return rt[side, pl.ds(first + (k - 1) * r, rows_out), :]

        low = jnp.where(half < pc, at(0, 0), jnp.where(half < 2 * pc, at(1, 0), at(2, 0)))
        up = 3 * pc - 128
        high = jnp.where(half < up, at(2, 1), jnp.where(half < up + pc, at(3, 1), at(4, 1)))
        return low, high

    grow = lax.broadcasted_iota(jnp.int32, (frows, 1), 0) + (base - LEAD)
    inside = (grow >= 0) & (grow < total)
    lrows = rows + 2 * LEAD

    def one_view(v, _):
        start = rows - LEAD + shifts[v]
        flag = flags[v]
        taps = [xf[pl.ds(start + (t - 1) * q, frows), :] for t in range(3)]
        stacked = jnp.concatenate([t.astype(BF16) for t in taps], axis=1)
        mixed = dot(stacked, kern[flag])
        feature = (taps[1] + jnp.maximum(mixed + cb_ref[...], 0.0)).astype(BF16)
        lw = dot(feature[:lrows], wide_left).astype(BF16).astype(F32)
        for side in range(2):
            part = lw[:, side * 128 : side * 128 + 128]
            rt[side, pl.ds(0, lrows), :] = jnp.where(inside[:lrows], part, FAR)
        low, high = skew(rows, LEAD)
        l5[v, 0] = low
        l5[v, 1] = high
        rw = dot(feature, wide_right).astype(BF16).astype(F32)
        for side in range(2):
            part = rw[:, side * 128 : side * 128 + 128]
            rt[side, pl.ds(0, frows), :] = jnp.where(inside, part, FAR)
        low, high = skew(near + 16, 8)
        r5[0] = low
        r5[1] = high
        for b in range(3):
            for side in range(2):
                moved = r5[side, pl.ds(8 + (b - 1) * r, near), :]
                r5b[v, b, :, side * 128 : side * 128 + 128] = moved.astype(BF16)
        return 0

    lax.fori_loop(0, views, one_view, 0)

    cols[...] = jnp.zeros_like(cols)
    span = BAND + TILE
    edge = 2 * TILE
    edge_row = lax.broadcasted_iota(jnp.int32, (edge, WIDE), 0)
    shift_row = lax.broadcasted_iota(jnp.int32, (rows, 128), 0)

    def group(g, moves):
        i0 = lax.rem(g, r) + OUT_ROWS * r * lax.div(g, r)
        nb = pl.multiple_of(lax.div(i0, TILE) * TILE, TILE)
        off = i0 - nb
        head_mask = jnp.where(edge_row - off < r, FAR, 0.0).astype(BF16)
        tail_mask = jnp.where(
            edge_row + (span - edge) - off >= BAND - r, FAR, 0.0
        ).astype(BF16)
        hidden = None
        for v in range(views):
            row = jnp.concatenate([l5[v, side, pl.ds(i0, 1), :] for side in range(2)], 1)
            row = jnp.broadcast_to(row, (TILE, WIDE)).astype(BF16)[None]
            parts = []
            for b in range(3):
                value = r5b[v, b, pl.ds(nb, span), :]
                if b == 0:
                    value = jnp.concatenate([value[:edge] + head_mask, value[edge:]], 0)
                if b == 2:
                    value = jnp.concatenate([value[:-edge], value[-edge:] + tail_mask], 0)
                value = jnp.maximum(value.reshape(span // TILE, TILE, WIDE) + row, 0)
                parts.append(value.reshape(span, WIDE))
            summed = dot(jnp.concatenate(parts, 1), wall[...])
            term = jnp.maximum(summed + bias, 0.0)
            hidden = term if hidden is None else hidden + term
        spread = jnp.where(target == i0, head_rows, 0.0).astype(BF16)
        cols[pl.ds(nb, span), :] += dot(hidden.astype(BF16), spread)
        delta = shift_row - i0
        mine = (delta == 0) | (delta == r) | (delta == 2 * r)
        return jnp.where(mine, i0, moves)

    per_class = lax.div(lax.div(rows + r - 1, r) + OUT_ROWS - 1, OUT_ROWS)
    moves = lax.fori_loop(0, r * per_class, group, jnp.zeros((rows, 128), jnp.int32))

    lanes = cols.shape[0]
    flat = cols[...].T[:rows]
    moves = jnp.concatenate([moves] * (lanes // 128), axis=1)
    bit = 1
    while bit < rows:
        flat = jnp.where((moves & bit) != 0, pltpu.roll(flat, lanes - bit, 1), flat)
        bit *= 2
    out_ref[...] = flat[:, :BAND] * (1.0 / views)


def per_device(
    bins,
    conv_weight,
    conv_bias,
    pair_left,
    pair_right,
    pair_weight,
    pair_bias,
    head,
    shifts,
    flags,
    dilations,
):
    rows, channels = bins.shape
    views = shifts.shape[0]
    pc = pair_left.shape[1]
    segments = lax.axis_size("seg")
    near = rows + BAND
    frows = near + 2 * LEAD
    blocks = 1 + -(-(near + LEAD + 3 * DMAX) // rows)
    vmem = pl.BlockSpec(memory_space=pltpu.VMEM)
    smem = pl.BlockSpec(memory_space=pltpu.SMEM)
    window = pl.pallas_call(
        functools.partial(gather_kernel, segments, blocks, rows),
        out_shape=jax.ShapeDtypeStruct((blocks * rows, channels), BF16),
        in_specs=[vmem],
        out_specs=vmem,
        scratch_shapes=[
            pltpu.SemaphoreType.DMA((blocks,)),
            pltpu.SemaphoreType.DMA((blocks,)),
            pltpu.SemaphoreType.DMA,
        ],
        compiler_params=pltpu.CompilerParams(collective_id=0, has_side_effects=True),
    )(bins)
    lanes = -(-near // 128) * 128
    return pl.pallas_call(
        functools.partial(pair_kernel, rows, segments),
        out_shape=jax.ShapeDtypeStruct((rows, BAND), F32),
        in_specs=[smem] * 3 + [vmem] * 8,
        out_specs=vmem,
        scratch_shapes=[
            pltpu.VMEM((blocks * rows, channels), F32),
            pltpu.VMEM((2, 3 * channels, channels), BF16),
            pltpu.VMEM((3 * WIDE, WIDE), BF16),
            pltpu.VMEM((2, frows + 16, 128), F32),
            pltpu.VMEM((2, near + 16, 128), F32),
            pltpu.VMEM((views, 3, near, WIDE), BF16),
            pltpu.VMEM((views, 2, rows, 128), F32),
            pltpu.VMEM((lanes, 128), F32),
        ],
        compiler_params=pltpu.CompilerParams(vmem_limit_bytes=60 * 1024 * 1024),
    )(
        shifts,
        flags,
        dilations,
        window,
        conv_weight,
        conv_bias.reshape(1, channels),
        pair_left,
        pair_right,
        pair_weight.reshape(9 * pc, pc),
        pair_bias.reshape(1, pc),
        head.reshape(1, pc),
    )


def solution(mesh):
    placed = (P(("groups", "seg"), None), P(), P(), P(), P(), P(), P(), P(), P(), P(), P())
    return jax.shard_map(
        per_device,
        mesh=mesh,
        in_specs=placed,
        out_specs=P(("groups", "seg"), None),
        check_vma=False,
    )
```

time: 357 us -> 33.7 us (0.09)
  local copies, waits for them, and re-layouts: 164 us -> 2.16 us
  matrix products: 145 us -> 0 us
  Pallas kernels: 0 us -> 31.2 us
  waiting for transfers between devices: 21.4 us -> 0 us
  starting transfers between devices: 11.1 us -> 0 us
  other arithmetic: 10.3 us -> 0 us
  between operations: 3.65 us -> 0.01 us
    dot_general x21 -> x0, matrix products: 145 us -> none  [the longest x12 76 us: view_step(): jnp.einsum('cid,bce->beid', row_piece, pair_weight[row_tap], preferred_el...]
    slice x28 -> x0, local copies, waits for them, and re-layouts: 106 us -> none  [the longest x8 91.1 us: view_step(): product[col_tap]]
    pallas_call x0 -> x2, Pallas kernels: none -> 31.2 us  [the longest x1 20.7 us: per_device(): pl.pallas_call(functools.partial(pair_kernel, rows, segments), out_shape=...]
    ppermute x8 -> x0, waiting for transfers between devices: 21.4 us -> none  [the longest x6 21.4 us: passed_along(): return lax.ppermute(block, axis, route)]
    reshape x5 -> x0, local copies, waits for them, and re-layouts: 16.8 us -> none  [the longest x4 16.7 us: view_step(): skewed = skewed.reshape(PAIR_CH, span, width + 1)[:, :, :BAND]]
    gather x36 -> x0, local copies, waits for them, and re-layouts: 15.1 us -> none
    another operation x8 -> x0, local copies, waits for them, and re-layouts: 14.7 us -> none  [view_step(): skewed = jnp.tile(right_cols, (1, span + 1))[:, :span * (width + 1)]]
    ppermute x8 -> x0, starting transfers between devices: 11.1 us -> none  [the longest x6 7.47 us: passed_along(): return lax.ppermute(block, axis, route)]
  transfers between devices with their start and end apart: 8 -> 0, of which waited for: 4 -> 0; matrix products, arithmetic and copies ran while one was open for 2% -> 0% of each run, Pallas kernels for 0% -> 0%
where the time goes in v1:
time: 33.7 us; the launch traced here: 33.4 us
  Pallas kernels  31.2 us (93%)
  local copies, waits for them, and re-layouts  2.16 us (6%)
    pallas_call x1, Pallas kernels, per_device(): pl.pallas_call(functools.partial(pair_kernel, rows, segments), out_shape=...  20.7 us
    pallas_call x1, Pallas kernels, per_device(): pl.pallas_call(functools.partial(gather_kernel, segments, blocks, rows),...  10.6 us
    unnamed x4, local copies, waits for them, and re-layouts  2.16 us

profile of v1, /device:TPU:0, one launch (start us, length us, event | category | flops | bytes accessed | tf_op | source)
XLA Modules:
  0.0 33.4 jit_solution(10489355159840681404)
XLA Ops:
  0.0 0.0 copy-start
  0.0 1.4 %copy.12.pleft_ref = bf16[128,48]{1,0:T(8,128)(2,1)} copy(bf16[128,48]{0,1:T(8,128)(2,1)} %param.14) | data formatting | bytes 24576 | tf_op args[3]
  1.4 0.0 copy-done
  1.4 0.7 %copy.13.pright_ref = bf16[128,48]{1,0:T(8,128)(2,1)} copy(bf16[128,48]{0,1:T(8,128)(2,1)S(1)} %copy-done) | data formatting | bytes 24576 | tf_op args[4]
  2.2 10.6 %shard_map.109.win_ref = bf16[608,128]{1,0:T(8,128)(2,1)} custom-call(bf16[32,128]{1,0:T(8,128)(2,1)} %x_ref.1), custom_call_target="tpu_custom_call" | custom-call | tf_op jit(solution)/shard_map/pallas_call | solution.py:289
  12.8 20.7 %shard_map.110 = f32[32,512]{1,0:T(8,128)} custom-call(s32[4]{0:T(128)} %shifts.1, s32[4]{0:T(128)} %flags.1, s32[2]{0:T(128)} %dilations.1, bf16[608,128]{1,0:T(8,128)(2,1)} %shard_map.109.win_ref, bf16[3,128,128]{2,1,0:T(8,128)(2,1)} %cw_ref.1, f32[1,128]{1,0:T(1,128)} %bitcast.5, bf16[128,48]{1,0:T(8,128)(2,1)} %copy.12.pleft_ref, ...), custom_call_target="tpu_custom_call" | custom-call | tf_op jit(solution)/shard_map/pallas_call | solution.py:302
Async XLA Ops:
  0.0 1.4 %copy-start = (bf16[128,48]{0,1:T(8,128)(2,1)S(1)}, bf16[128,48]{0,1:T(8,128)(2,1)}, u32[]{:S(2)}) copy-start(bf16[128,48]{0,1:T(8,128)(2,1)} %param.15) | copy-start | bytes 36868

commit v2 on v1

--- a/solution.py
+++ b/solution.py
@@ -91,6 +91,10 @@
 
 def dot(a, b, **kw):
     return jnp.dot(a, b, preferred_element_type=F32, **kw)
+
+
+def dot_t(a, b):
+    return lax.dot_general(a, b, (((0,), (0,)), ((), ())), preferred_element_type=F32)
 
 
 def pair_kernel(
@@ -118,7 +122,7 @@
     cols,
 ):
     channels = win_ref.shape[1]
-    pc = pleft_ref.shape[1]
+    pc = pleft_ref.shape[0]
     views = shifts.shape[0]
     total = rows * segments
     base = lax.axis_index("seg") * rows
@@ -141,8 +145,8 @@
     spots = [jnp.where(lane - chan == k * pc, 1.0, 0.0) for k in range(IN_ROWS)]
     tiler_f = sum(spots[1:], spots[0])
     tiler = tiler_f.astype(BF16)
-    wide_left = dot(pleft_ref[...], tiler).astype(BF16)
-    wide_right = dot(pright_ref[...], tiler).astype(BF16)
+    wide_left = dot_t(pleft_ref[...], tiler).astype(BF16)
+    wide_right = dot_t(pright_ref[...], tiler).astype(BF16)
     placed = [dot(pw_ref[...], spots[o].astype(BF16)) for o in range(OUT_ROWS)]
     for b in range(3):
         for k in range(IN_ROWS):
@@ -322,8 +326,8 @@
         window,
         conv_weight,
         conv_bias.reshape(1, channels),
-        pair_left,
-        pair_right,
+        pair_left.T,
+        pair_right.T,
         pair_weight.reshape(9 * pc, pc),
         pair_bias.reshape(1, pc),
         head.reshape(1, pc),

time: 33.7 us -> 31.5 us (0.935)
  local copies, waits for them, and re-layouts: 2.16 us -> 0 us
    unnamed x4 -> x0, local copies, waits for them, and re-layouts: 2.16 us -> none
where the time goes in v2:
time: 31.5 us; the launch traced here: 31.4 us
  Pallas kernels  31.3 us (99%)
    pallas_call x1, Pallas kernels, per_device(): pl.pallas_call(functools.partial(pair_kernel, rows, segments), out_shape=...  20.8 us
    pallas_call x1, Pallas kernels, per_device(): pl.pallas_call(functools.partial(gather_kernel, segments, blocks, rows),...  10.6 us

profile of v2, /device:TPU:0, one launch (start us, length us, event | category | flops | bytes accessed | tf_op | source)
XLA Modules:
  0.0 31.4 jit_solution(7213719776016793960)
XLA Ops:
  0.0 10.6 %shard_map.109.win_ref = bf16[608,128]{1,0:T(8,128)(2,1)} custom-call(bf16[32,128]{1,0:T(8,128)(2,1)} %x_ref.1), custom_call_target="tpu_custom_call" | custom-call | tf_op jit(solution)/shard_map/pallas_call | solution.py:293
  10.6 20.8 %shard_map.110 = f32[32,512]{1,0:T(8,128)} custom-call(s32[4]{0:T(128)} %shifts.1, s32[4]{0:T(128)} %flags.1, s32[2]{0:T(128)} %dilations.1, bf16[608,128]{1,0:T(8,128)(2,1)} %shard_map.109.win_ref, bf16[3,128,128]{2,1,0:T(8,128)(2,1)} %cw_ref.1, f32[1,128]{1,0:T(1,128)} %bitcast.9, bf16[48,128]{1,0:T(8,128)(2,1)} %bitcast.7, bf16[48,128]{1,0:T(8,128)(2,1)} %bitcast.8, ...), custom_call_target="tpu_custom_call" | custom-call | tf_op jit(solution)/shard_map/pallas_call | solution.py:306

commit v3 on v2

--- a/solution.py
+++ b/solution.py
@@ -115,11 +115,9 @@
     xf,
     kern,
     wall,
-    rt,
-    r5,
-    r5b,
     l5,
     cols,
+    *per_view,
 ):
     channels = win_ref.shape[1]
     pc = pleft_ref.shape[0]
@@ -177,7 +175,7 @@
 
     half = lax.broadcasted_iota(jnp.int32, (1, 128), 1)
 
-    def skew(rows_out, first):
+    def skew(rt, rows_out, first):
         def at(k, side):
             return rt[side, pl.ds(first + (k - 1) * r, rows_out), :]
 
@@ -190,7 +188,8 @@
     inside = (grow >= 0) & (grow < total)
     lrows = rows + 2 * LEAD
 
-    def one_view(v, _):
+    def one_view(v):
+        lt, rt, r5, r5b = per_view[4 * v : 4 * v + 4]
         start = rows - LEAD + shifts[v]
         flag = flags[v]
         taps = [xf[pl.ds(start + (t - 1) * q, frows), :] for t in range(3)]
@@ -200,24 +199,24 @@
         lw = dot(feature[:lrows], wide_left).astype(BF16).astype(F32)
         for side in range(2):
             part = lw[:, side * 128 : side * 128 + 128]
-            rt[side, pl.ds(0, lrows), :] = jnp.where(inside[:lrows], part, FAR)
-        low, high = skew(rows, LEAD)
+            lt[side] = jnp.where(inside[:lrows], part, FAR)
+        low, high = skew(lt, rows, LEAD)
         l5[v, 0] = low
         l5[v, 1] = high
         rw = dot(feature, wide_right).astype(BF16).astype(F32)
         for side in range(2):
             part = rw[:, side * 128 : side * 128 + 128]
             rt[side, pl.ds(0, frows), :] = jnp.where(inside, part, FAR)
-        low, high = skew(near + 16, 8)
+        low, high = skew(rt, near + 16, 8)
         r5[0] = low
         r5[1] = high
         for b in range(3):
             for side in range(2):
                 moved = r5[side, pl.ds(8 + (b - 1) * r, near), :]
-                r5b[v, b, :, side * 128 : side * 128 + 128] = moved.astype(BF16)
-        return 0
-
-    lax.fori_loop(0, views, one_view, 0)
+                r5b[b, :, side * 128 : side * 128 + 128] = moved.astype(BF16)
+
+    for v in range(views):
+        one_view(v)
 
     cols[...] = jnp.zeros_like(cols)
     span = BAND + TILE
@@ -239,7 +238,7 @@
             row = jnp.broadcast_to(row, (TILE, WIDE)).astype(BF16)[None]
             parts = []
             for b in range(3):
-                value = r5b[v, b, pl.ds(nb, span), :]
+                value = per_view[4 * v + 3][b, pl.ds(nb, span), :]
                 if b == 0:
                     value = jnp.concatenate([value[:edge] + head_mask, value[edge:]], 0)
                 if b == 2:
@@ -312,12 +311,16 @@
             pltpu.VMEM((blocks * rows, channels), F32),
             pltpu.VMEM((2, 3 * channels, channels), BF16),
             pltpu.VMEM((3 * WIDE, WIDE), BF16),
+            pltpu.VMEM((views, 2, rows, 128), F32),
+            pltpu.VMEM((lanes, 128), F32),
+        ]
+        + [
+            pltpu.VMEM((2, rows + 2 * LEAD, 128), F32),
             pltpu.VMEM((2, frows + 16, 128), F32),
             pltpu.VMEM((2, near + 16, 128), F32),
-            pltpu.VMEM((views, 3, near, WIDE), BF16),
-            pltpu.VMEM((views, 2, rows, 128), F32),
-            pltpu.VMEM((lanes, 128), F32),
-        ],
+            pltpu.VMEM((3, near, WIDE), BF16),
+        ]
+        * views,
         compiler_params=pltpu.CompilerParams(vmem_limit_bytes=60 * 1024 * 1024),
     )(
         shifts,

time: 31.5 us -> 30.2 us (0.959)
  Pallas kernels: 31.3 us -> 30 us
    pallas_call x1, Pallas kernels: 20.8 us -> 19.4 us  [per_device(): pl.pallas_call(functools.partial(pair_kernel, rows, segments), out_shape=...]
where the time goes in v3:
time: 30.2 us; the launch traced here: 30 us
  Pallas kernels  30 us (99%)
    pallas_call x1, Pallas kernels, per_device(): pl.pallas_call(functools.partial(pair_kernel, rows, segments), out_shape=...  19.4 us
    pallas_call x1, Pallas kernels, per_device(): pl.pallas_call(functools.partial(gather_kernel, segments, blocks, rows),...  10.6 us

profile of v3, /device:TPU:0, one launch (start us, length us, event | category | flops | bytes accessed | tf_op | source)
XLA Modules:
  0.0 30.0 jit_solution(14925117364428035161)
XLA Ops:
  0.0 10.6 %shard_map.109.win_ref = bf16[608,128]{1,0:T(8,128)(2,1)} custom-call(bf16[32,128]{1,0:T(8,128)(2,1)} %x_ref.1), custom_call_target="tpu_custom_call" | custom-call | tf_op jit(solution)/shard_map/pallas_call | solution.py:292
  10.6 19.4 %shard_map.110 = f32[32,512]{1,0:T(8,128)} custom-call(s32[4]{0:T(128)} %shifts.1, s32[4]{0:T(128)} %flags.1, s32[2]{0:T(128)} %dilations.1, bf16[608,128]{1,0:T(8,128)(2,1)} %shard_map.109.win_ref, bf16[3,128,128]{2,1,0:T(8,128)(2,1)} %cw_ref.1, f32[1,128]{1,0:T(1,128)} %bitcast.9, bf16[48,128]{1,0:T(8,128)(2,1)} %bitcast.7, bf16[48,128]{1,0:T(8,128)(2,1)} %bitcast.8, ...), custom_call_target="tpu_custom_call" | custom-call | tf_op jit(solution)/shard_map/pallas_call | solution.py:305

commit v4 on v3

--- a/solution.py
+++ b/solution.py
@@ -212,7 +212,10 @@
         r5[1] = high
         for b in range(3):
             for side in range(2):
-                moved = r5[side, pl.ds(8 + (b - 1) * r, near), :]
+                if b == 1:
+                    moved = (low, high)[side][8 : 8 + near]
+                else:
+                    moved = r5[side, pl.ds(8 + (b - 1) * r, near), :]
                 r5b[b, :, side * 128 : side * 128 + 128] = moved.astype(BF16)
 
     for v in range(views):

time: 30.2 us -> 30.1 us (level)
  no operation moved by 1% of the time
where the time goes in v4:
time: 30.1 us; the launch traced here: 29.9 us
  Pallas kernels  29.9 us (99%)
    pallas_call x1, Pallas kernels, per_device(): pl.pallas_call(functools.partial(pair_kernel, rows, segments), out_shape=...  19.3 us
    pallas_call x1, Pallas kernels, per_device(): pl.pallas_call(functools.partial(gather_kernel, segments, blocks, rows),...  10.6 us

profile of v4, /device:TPU:0, one launch (start us, length us, event | category | flops | bytes accessed | tf_op | source)
XLA Modules:
  0.0 29.9 jit_solution(9788543534984970578)
XLA Ops:
  0.0 10.6 %shard_map.109.win_ref = bf16[608,128]{1,0:T(8,128)(2,1)} custom-call(bf16[32,128]{1,0:T(8,128)(2,1)} %x_ref.1), custom_call_target="tpu_custom_call" | custom-call | tf_op jit(solution)/shard_map/pallas_call | solution.py:295
  10.6 19.3 %shard_map.110 = f32[32,512]{1,0:T(8,128)} custom-call(s32[4]{0:T(128)} %shifts.1, s32[4]{0:T(128)} %flags.1, s32[2]{0:T(128)} %dilations.1, bf16[608,128]{1,0:T(8,128)(2,1)} %shard_map.109.win_ref, bf16[3,128,128]{2,1,0:T(8,128)(2,1)} %cw_ref.1, f32[1,128]{1,0:T(1,128)} %bitcast.9, bf16[48,128]{1,0:T(8,128)(2,1)} %bitcast.7, bf16[48,128]{1,0:T(8,128)(2,1)} %bitcast.8, ...), custom_call_target="tpu_custom_call" | custom-call | tf_op jit(solution)/shard_map/pallas_call | solution.py:308
